TPU v7x, 512 devices: a whole 4x8x8 slice. The times are simulated.
512 devices in a mesh: ctx: 32 (over y, z_hi), head: 16 (over z_lo, x, core).
Axes of the slice: x: 4, y: 8, z: 8 (z_hi: 4, z_lo: 2; z = z_hi * 2 + z_lo), core: 2. Of those that a mesh axis runs over, the one named last changes fastest.
Arguments:
- queries: bfloat16 [16, 8192, 1024], P('head', 'ctx'), may hold values from -6 to 6
- keys: bfloat16 [16, 8192, 128], P('head', 'ctx'), may hold values from -6 to 6
- values: bfloat16 [16, 8192, 128], P('head', 'ctx'), may hold values from -6 to 6
- documents: int32 [16, 8192], P('head', 'ctx'), may hold values from 0 to 3, never falling along the last dimension, each value on 1 to 4096 neighbouring positions
Outputs:
- tokens_out: bfloat16 [16, 8192, 1024], P(None, ('ctx', 'head'))
- log_sums: float32 [16, 8, 8192], P('head', None, 'ctx')
Inputs may be any that keep to these rules, and one draw needn't show every extreme that they name: `documents`: each row's ids never fall along positions; each document holds at most half of the 8192 positions.
All inputs are finite; a program needn't handle non-finite values.
Results may differ from a plain program's by a relative error of at most 0.0075.
Values may be sent and summed in bfloat16 or wider, within the bound.
No kernel may reach another device: no remote copies, remote signals or barrier semaphores. Data moves between devices by JAX's collectives and lax.ppermute only.
A program may use at most 64 MiB of HBM per device.

v0:
```python
import jax
import jax.numpy as jnp
from jax import lax
from jax.sharding import PartitionSpec as P

NEG_FILL = -1e30


def attend_block(
    block_state,
    query_rows,
    query_pos,
    query_doc,
    key_rows,
    value_rows,
    key_pos,
    key_doc,
    score_scale,
):
    run_max, run_total, run_acc = block_state
    scores = (
        jnp.einsum("uqgd,ukd->ugqk", query_rows, key_rows, preferred_element_type=jnp.float32)
        * score_scale
    )
    visible = (key_pos[None, None, :] <= query_pos[None, :, None]) & (
        key_doc[:, None, :] == query_doc[:, :, None]
    )
    scores = jnp.where(visible[:, None], scores, NEG_FILL)
    new_max = jnp.maximum(run_max, jnp.max(scores, axis=3))
    weights = jnp.where(visible[:, None], jnp.exp(scores - new_max[..., None]), 0.0)
    factor = jnp.exp(run_max - new_max)
    new_total = factor * run_total + jnp.sum(weights, axis=3)
    rounded = weights.astype(jnp.bfloat16)
    mixed_rows = jnp.einsum(
        "ugqk,ukd->uqgd", rounded, value_rows, preferred_element_type=jnp.float32
    )
    new_acc = jnp.swapaxes(factor, 1, 2)[..., None] * run_acc + mixed_rows
    return (new_max, new_total, new_acc)


def attend_rows(rows, row_docs, row_pos, keys, values, documents):
    unit_count, shard_rows, row_width = rows.shape
    head_dim = keys.shape[2]
    groups = row_width // head_dim
    block_rows = shard_rows // 2
    score_scale = 1.0 / head_dim**0.5
    query_list = []
    pos_list = []
    doc_list = []
    init_list = []
    for block_index in range(2):
        lower = block_index * block_rows
        query_list.append(
            rows[:, lower : lower + block_rows].reshape(unit_count, block_rows, groups, head_dim)
        )
        pos_list.append(row_pos[lower : lower + block_rows])
        doc_list.append(row_docs[:, lower : lower + block_rows])
        init_list.append(
            (
                jnp.full((unit_count, groups, block_rows), NEG_FILL, jnp.float32),
                jnp.zeros((unit_count, groups, block_rows), jnp.float32),
                jnp.zeros((unit_count, block_rows, groups, head_dim), jnp.float32),
            )
        )
    key_all = lax.all_gather(keys, "ctx", axis=1, tiled=True)
    value_all = lax.all_gather(values, "ctx", axis=1, tiled=True)
    doc_all = lax.all_gather(documents, "ctx", axis=1, tiled=True)
    piece_blocks = key_all.shape[1] // shard_rows

    def key_step(step_index, inner_carry):
        offset = step_index * shard_rows
        key_rows = lax.dynamic_slice_in_dim(key_all, offset, shard_rows, 1)
        value_rows = lax.dynamic_slice_in_dim(value_all, offset, shard_rows, 1)
        key_doc = lax.dynamic_slice_in_dim(doc_all, offset, shard_rows, 1)
        key_pos = offset + jnp.arange(shard_rows, dtype=jnp.int32)
        updated = []
        for block_index in range(2):
            query_pos = pos_list[block_index]
            query_doc = doc_list[block_index]
            query_rows = query_list[block_index]
            needed = (key_pos[0] <= query_pos[-1]) & jnp.any(key_doc[:, -1] >= query_doc[:, 0])

            def compute(
                block_state, query_rows=query_rows, query_pos=query_pos, query_doc=query_doc
            ):
                return attend_block(
                    block_state,
                    query_rows,
                    query_pos,
                    query_doc,
                    key_rows,
                    value_rows,
                    key_pos,
                    key_doc,
                    score_scale,
                )

            def keep(block_state):
                return block_state

            updated.append(lax.cond(needed, compute, keep, inner_carry[block_index]))
        return tuple(updated)

    final = lax.fori_loop(0, piece_blocks, key_step, tuple(init_list))
    out_parts = []
    lse_parts = []
    for block_index in range(2):
        run_max, run_total, run_acc = final[block_index]
        normed = (run_acc / jnp.swapaxes(run_total, 1, 2)[..., None]).astype(jnp.bfloat16)
        out_parts.append(normed.reshape(unit_count, block_rows, row_width))
        lse_parts.append(run_max + jnp.log(run_total))
    return (jnp.concatenate(out_parts, axis=1), jnp.concatenate(lse_parts, axis=2))


def body(queries, keys, values, documents):
    my_place = lax.axis_index("ctx")
    shard_rows = queries.shape[1]
    row_pos = my_place * shard_rows + jnp.arange(shard_rows, dtype=jnp.int32)
    own_out, own_lse = attend_rows(queries, documents, row_pos, keys, values, documents)
    tokens_out = lax.all_to_all(own_out, "head", split_axis=1, concat_axis=0, tiled=True)
    return (tokens_out, own_lse)


def solution(mesh):
    in_specs = (
        P("head", "ctx", None),
        P("head", "ctx", None),
        P("head", "ctx", None),
        P("head", "ctx"),
    )
    out_specs = (P(None, ("ctx", "head"), None), P("head", None, "ctx"))
    return jax.shard_map(body, mesh=mesh, in_specs=in_specs, out_specs=out_specs, check_vma=False)
```

profile of v0, /device:TPU:48, one launch (start us, length us, event | category | flops | bytes accessed | tf_op | source)
XLA Modules:
  0.0 484.4 jit_solution(9185862164013778185)
XLA Ops:
  7.2 0.7 all-gather.3.cloned.1.call-update
  8.0 0.7 all-gather.5.cloned.1.call-update
  8.7 1.1 fusion.33
  10.5 75.9 %all_gather.9 = s32[1,8192]{1,0:T(1,128)S(1)} all-gather(s32[1,256]{1,0:T(1,128)S(1)} %copy-done), channel_id=1, replica_groups=mesh['ctx'=32,'head'=16] {'ctx'}, dimensions={1}, use_global_device_ids=true | all-gather | bytes 33792 | tf_op jit(solution)/shard_map/all_gather | solution.py:67
  86.4 14.4 %all-gather.3.cloned.1.call-done = bf16[1,8192,128]{2,1,0:T(8,128)(2,1)} async-done(((bf16[1,256,128]{2,1,0:T(8,128)(2,1)}), bf16[1,8192,128]{2,1,0:T(8,128)(2,1)}) %all-gather.3.cloned.1.call-update) | async-done | bytes 2097168 | tf_op jit(solution)/shard_map/all_gather | solution.py:65
  100.8 86.0 %all-gather.5.cloned.1.call-done = bf16[1,8192,128]{2,1,0:T(8,128)(2,1)} async-done(((bf16[1,256,128]{2,1,0:T(8,128)(2,1)}), bf16[1,8192,128]{2,1,0:T(8,128)(2,1)}) %all-gather.5.cloned.1.call-update) | async-done | bytes 2097168 | tf_op jit(solution)/shard_map/all_gather | solution.py:66
  186.9 236.7 %while.23 = (s32[]{:T(128)}, f32[1,8,128]{2,1,0:T(8,128)S(1)}, f32[1,8,128]{2,1,0:T(8,128)S(1)}, f32[1,128,8,128]{3,1,2,0:T(8,128)S(1)}, f32[1,8,128]{2,1,0:T(8,...) while((s32[]{:T(128)}, f32[1,8,128]{2,1,0:T(8,128)S(1)}, ...), condition=%wide.region_9.10_spmd, body=%wide.region_0.9_spmd.sunk | while | flops 273881344 | bytes 9840231 | solution.py:104
  186.9 0.9 constant_dynamic-slice_fusion.7
  194.0 0.9 constant_dynamic-slice_fusion.7
  198.5 0.6 slice.78
  201.1 0.9 constant_dynamic-slice_fusion.7
  208.2 0.9 constant_dynamic-slice_fusion.7
  212.7 0.6 slice.78
  215.3 0.9 constant_dynamic-slice_fusion.7
  219.8 0.6 slice.78
  222.4 0.9 constant_dynamic-slice_fusion.7
  229.5 0.9 constant_dynamic-slice_fusion.7
  234.0 0.6 slice.78
  236.6 0.9 constant_dynamic-slice_fusion.7
  243.7 0.9 constant_dynamic-slice_fusion.7
  250.8 0.9 constant_dynamic-slice_fusion.7
  255.3 0.6 slice.78
  257.9 0.9 constant_dynamic-slice_fusion.7
  265.0 0.9 constant_dynamic-slice_fusion.7
  272.1 0.9 constant_dynamic-slice_fusion.7
  276.6 0.6 slice.78
  279.2 0.9 constant_dynamic-slice_fusion.7
  286.3 0.9 constant_dynamic-slice_fusion.7
  290.8 0.6 slice.78
  293.4 0.9 constant_dynamic-slice_fusion.7
  300.5 0.9 constant_dynamic-slice_fusion.7
  307.6 0.9 constant_dynamic-slice_fusion.7
  312.1 0.6 slice.78
  314.7 0.9 constant_dynamic-slice_fusion.7
  321.8 0.9 constant_dynamic-slice_fusion.7
  328.9 0.9 constant_dynamic-slice_fusion.7
  333.4 0.6 slice.78
  336.0 0.9 constant_dynamic-slice_fusion.7
  340.5 1.2 conditional.5
  341.7 0.6 slice.78
  344.2 1.2 conditional.4
  345.5 0.9 constant_dynamic-slice_fusion.7
  349.9 1.2 conditional.5
  353.7 1.2 conditional.4
  355.0 0.9 constant_dynamic-slice_fusion.7
  359.4 1.2 conditional.5
  360.7 0.6 slice.78
  363.2 1.2 conditional.4
  364.5 0.9 constant_dynamic-slice_fusion.7
  368.9 1.2 conditional.5
  372.7 1.2 conditional.4
  373.9 0.9 constant_dynamic-slice_fusion.7
  381.0 0.9 constant_dynamic-slice_fusion.7
  388.1 0.9 constant_dynamic-slice_fusion.7
  395.2 0.9 constant_dynamic-slice_fusion.7
  402.3 0.9 constant_dynamic-slice_fusion.7
  409.4 0.9 constant_dynamic-slice_fusion.7
  416.5 0.9 constant_dynamic-slice_fusion.7
  424.2 1.0 copy.34
  425.8 3.7 reduce.4
  429.5 1.2 reshape.263
  430.6 34.5 %all-to-all-start = ((bf16[16,2,8192]{2,1,0:T(2,128)(2,1)}), bf16[16,2,8192]{2,1,0:T(2,128)(2,1)S(1)}, u32[]{:S(2)}, u32[]{:S(2)}) async-start(bf16[16,2,8192]{2,1,0:T(2,128)(2,1)} %reshape.263), calls=%async_computation | async-start | bytes 1048576 | tf_op jit(solution)/shard_map/all_to_all | solution.py:120
  465.8 10.2 %all-to-all-done = bf16[16,2,8192]{2,1,0:T(2,128)(2,1)S(1)} async-done(((bf16[16,2,8192]{2,1,0:T(2,128)(2,1)}), bf16[16,2,8192]{2,1,0:T(2,128)(2,1)S(1)}, u32[]{:S(2)}, u32[]{:S(2)}) %all-to-all-start) | async-done | bytes 524320 | tf_op jit(solution)/shard_map/all_to_all | solution.py:120
  476.6 1.0 copy.37
  (319 shorter events, 81.3 us)
Async XLA Ops:
  7.2 3.3 copy-start
  7.2 93.6 %all-gather.3.cloned.1.call-start = ((), (), s32[]{:S(2)}) async-start(), calls=%async_computation.1 | async-start | bytes 2162688 | tf_op jit(solution)/shard_map/all_gather | solution.py:65
  7.9 178.8 %all-gather.5.cloned.1.call-start = ((), (), s32[]{:S(2)}) async-start(), calls=%async_computation.2 | async-start | bytes 2162688 | tf_op jit(solution)/shard_map/all_gather | solution.py:66
  430.6 45.4 %all-to-all-start = ((bf16[16,2,8192]{2,1,0:T(2,128)(2,1)}), bf16[16,2,8192]{2,1,0:T(2,128)(2,1)S(1)}, u32[]{:S(2)}, u32[]{:S(2)}) async-start(bf16[16,2,8192]{2,1,0:T(2,128)(2,1)} %reshape.263), calls=%async_computation | async-start | bytes 1048576 | tf_op jit(solution)/shard_map/all_to_all | solution.py:120
Sparse Core Ops, SparseCore 0:
  11.2 89.5 all-gather.2
  104.0 82.7 all-gather.4
where the time goes:
time: 488 us; the launch traced here: 484 us
  loops' own time  124 us (25%)
  waiting for transfers between devices  112 us (23%)
  local copies, waits for them, and re-layouts  89.9 us (18%)
  blocking collectives  75.9 us (16%)
  starting transfers between devices  34.6 us (7%)
  other arithmetic  27.5 us (6%)
  between operations  14.2 us (3%)
  matrix products  6.38 us (1%)
    another operation x1, loops' own time, attend_rows(): final = lax.fori_loop(0, piece_blocks, key_step, tuple(init_list))  123 us
    all_gather x1, waiting for transfers between devices, attend_rows(): value_all = lax.all_gather(values, 'ctx', axis=1, tiled=True)  86 us
    all_gather x1, blocking collectives, attend_rows(): doc_all = lax.all_gather(documents, 'ctx', axis=1, tiled=True)  75.9 us
    slice x64, local copies, waits for them, and re-layouts, key_step(): query_pos[-1]  38.4 us
    all_to_all x1, starting transfers between devices, body(): lax.all_to_all(own_out, 'head', split_axis=1, concat_axis=0, tiled=True)  34.5 us
    dynamic_slice x32, local copies, waits for them, and re-layouts, key_step(): value_rows = lax.dynamic_slice_in_dim(value_all, offset, shard_rows, 1)  28.4 us
    ge x32, other arithmetic, key_step(): key_doc[:, -1] >= query_doc[:, 0]  20.1 us
    slice x32, local copies, waits for them, and re-layouts, key_step(): key_pos[0] <= query_pos[-1]  16.4 us
  transfers between devices with their start and end apart: 3, of which 3 were waited for; matrix products, arithmetic and copies ran while one was open for 0% of the time, Pallas kernels for 0%

commit v1 on v0

v1 whole, which is shorter than its diff:
```python
import functools

import jax
import jax.numpy as jnp
import numpy as np
from jax import lax
from jax.experimental import pallas as pl
from jax.experimental.pallas import tpu as pltpu
from jax.sharding import PartitionSpec as P

NEG_FILL = -1e30
ROWS = 4
EXTRA = 8


def attention_kernel(
    scale, shard, groups, head_dim, q_ref, doc_ref, own_ref, row_hbm, near1_hbm, near2_hbm, far_hbm,
    out_ref, lse_ref, buf, key_docs, flags, run_max, run_acc, sems,
):
    place = lax.axis_index("ctx")
    row = place // ROWS
    col = lax.rem(place, ROWS)
    factor = scale * np.log2(np.e)
    sources = (row_hbm, near1_hbm, near2_hbm, far_hbm)
    copies = []
    first = 0
    for index, source in enumerate(sources):
        count = source.shape[0]
        copies.append(
            pltpu.make_async_copy(source, buf.at[pl.ds(first, count)], sems.at[index])
        )
        first += count
    for copy in copies:
        copy.start()

    doc_row = doc_ref[...].astype(jnp.float32)
    query_docs = jnp.transpose(jnp.broadcast_to(doc_row, (128, shard)))
    first_doc = jnp.min(doc_row)
    last_doc = jnp.max(doc_row)

    def attend(keys, vals, lines, fresh):
        vals = jnp.concatenate([vals, jnp.ones_like(vals)], axis=1)
        tiles = keys.shape[0] // 128
        for g in range(groups):
            scores = lax.dot_general(
                q_ref[:, g * head_dim : (g + 1) * head_dim],
                keys,
                (((1,), (1,)), ((), ())),
                preferred_element_type=jnp.float32,
            )
            if lines:
                parts = []
                for j in range(tiles):
                    at = j * 128 % shard
                    keep = query_docs == lines[j * 128 // shard][:, at : at + 128]
                    if fresh:
                        key_at = lax.broadcasted_iota(jnp.int32, (shard, 128), 1) + j * 128
                        keep = keep & (key_at <= lax.broadcasted_iota(jnp.int32, (shard, 128), 0))
                    parts.append(jnp.where(keep, scores[:, j * 128 : (j + 1) * 128], NEG_FILL))
                scores = jnp.concatenate(parts, axis=1)
            top = jnp.max(scores, axis=1, keepdims=True)
            if fresh:
                new_max = jnp.broadcast_to(top, (shard, 128))
            else:
                old_max = run_max[g]
                new_max = jnp.maximum(old_max, top)
            parts = [
                jnp.exp2((scores[:, j * 128 : (j + 1) * 128] - new_max) * factor).astype(jnp.bfloat16)
                for j in range(tiles)
            ]
            weights = jnp.concatenate(parts, axis=1)
            mixed = jnp.dot(weights, vals, preferred_element_type=jnp.float32)
            if fresh:
                run_acc[g] = mixed
            else:
                fade = jnp.exp2((old_max - new_max) * factor)
                run_acc[g, :, :head_dim] = run_acc[g, :, :head_dim] * fade + mixed[:, :head_dim]
                run_acc[g, :, head_dim:] = run_acc[g, :, head_dim:] * fade + mixed[:, head_dim:]
            run_max[g] = new_max

    def attend_pair(pair, masked):
        slots = (2 * pair, 2 * pair + 1)
        keys = jnp.concatenate([buf[slot, :shard, :head_dim] for slot in slots], axis=0)
        vals = jnp.concatenate([buf[slot, :shard, head_dim:] for slot in slots], axis=0)
        attend(keys, vals, [key_docs[slot, 0:1, :] for slot in slots] if masked else [], False)

    attend(own_ref[0, :shard, :head_dim], own_ref[0, :shard, head_dim:], [doc_row], True)

    back = [0] * ROWS + [1] * ROWS + [2] * ROWS + [3, 4] * ROWS
    pairs = len(back) // 2
    for copy in copies:
        copy.wait()
    lines = []
    for slot, rows_back in enumerate(back):
        line = buf[slot, shard : shard + EXTRA, :].astype(jnp.float32)[0:1, :]
        line = jnp.where(row >= rows_back if rows_back else slot < col, line, -1.0)
        key_docs[slot] = jnp.broadcast_to(line, (8, shard))
        lines.append(line)
    for pair in range(pairs):
        low = jnp.min(jnp.minimum(lines[2 * pair], lines[2 * pair + 1]))
        high = jnp.max(jnp.maximum(lines[2 * pair], lines[2 * pair + 1]))
        flags[pair] = jnp.where(high >= first_doc, jnp.where(low == last_doc, 1, 2), 0)

    @pl.loop(0, pairs)
    def _(pair):
        flag = flags[pair]

        @pl.when(flag == 1)
        def _():
            attend_pair(pair, False)

        @pl.when(flag == 2)
        def _():
            attend_pair(pair, True)

    lane = lax.broadcasted_iota(jnp.int32, (shard, 128), 1)
    sums = jnp.zeros((shard, 128), jnp.float32)
    for g in range(groups):
        total = run_acc[g, :, head_dim:]
        out_ref[:, g * head_dim : (g + 1) * head_dim] = (
            run_acc[g, :, :head_dim] / total
        ).astype(jnp.bfloat16)
        sums = jnp.where(lane == g, run_max[g] * scale + jnp.log(total), sums)
    lse_ref[...] = jnp.transpose(sums)[:groups, :]


def attend_rows(queries, docs, own, row, near1, near2, far, head_dim):
    shard, width = queries.shape
    groups = width // head_dim
    slots = row.shape[0] + near1.shape[0] + near2.shape[0] + far.shape[0]
    anywhere = pl.BlockSpec(memory_space=pl.ANY)
    vmem = pl.BlockSpec(memory_space=pltpu.VMEM)
    work = shard * width * slots * shard
    return pl.pallas_call(
        functools.partial(attention_kernel, 1.0 / head_dim**0.5, shard, groups, head_dim),
        out_shape=(
            jax.ShapeDtypeStruct((shard, width), jnp.bfloat16),
            jax.ShapeDtypeStruct((groups, shard), jnp.float32),
        ),
        in_specs=[vmem, vmem, vmem] + [anywhere] * 4,
        out_specs=(vmem, vmem),
        scratch_shapes=[
            pltpu.VMEM((slots, shard + EXTRA, 2 * head_dim), jnp.bfloat16),
            pltpu.VMEM((slots, 8, shard), jnp.float32),
            pltpu.SMEM((16,), jnp.int32),
            pltpu.VMEM((groups, shard, 128), jnp.float32),
            pltpu.VMEM((groups, shard, 2 * head_dim), jnp.float32),
            pltpu.SemaphoreType.DMA((4,)),
        ],
        compiler_params=pltpu.CompilerParams(vmem_limit_bytes=40 << 20),
        cost_estimate=pl.CostEstimate(
            flops=4 * work, bytes_accessed=4 << 20, transcendentals=work // head_dim
        ),
        name="attention",
    )(queries, docs, own, row, near1, near2, far)


def shift(array, rows_on, grid_rows):
    count = grid_rows * ROWS
    pairs = [(place, (place + rows_on * ROWS) % count) for place in range(count)]
    return lax.ppermute(array, "ctx", pairs)


def row_gather(array, grid_rows):
    groups = [[r * ROWS + c for c in range(ROWS)] for r in range(grid_rows)]
    sent = jnp.broadcast_to(array[None], (ROWS, *array.shape))
    got = lax.all_to_all(sent, "ctx", split_axis=0, concat_axis=0, tiled=True, axis_index_groups=groups)
    return got.reshape(ROWS * array.shape[0], *array.shape[1:])


def body(grid_rows, queries, keys, values, documents):
    head_dim = keys.shape[2]
    packed = jnp.concatenate([keys[0], values[0]], axis=1)
    doc_rows = jnp.pad(documents.astype(jnp.bfloat16), ((0, EXTRA - 1), (0, 0)))
    packed = jnp.concatenate([packed, doc_rows], axis=0)[None]
    far3 = shift(packed, 3, grid_rows)
    far4 = shift(packed, 4, grid_rows)
    row = row_gather(packed, grid_rows)
    near1 = shift(row, 1, grid_rows)
    near2 = shift(near1, 1, grid_rows)
    far = row_gather(jnp.concatenate([far3, far4], axis=0), grid_rows)
    out, lse = attend_rows(queries[0], documents, packed, row, near1, near2, far, head_dim)
    parts = lax.axis_size("head")
    blocks = out.reshape(parts, out.shape[0] // parts, out.shape[1])
    tokens = lax.all_to_all(blocks, "head", split_axis=0, concat_axis=0, tiled=True)
    return (tokens, lse[None])


def solution(mesh):
    in_specs = (
        P("head", "ctx", None),
        P("head", "ctx", None),
        P("head", "ctx", None),
        P("head", "ctx"),
    )
    out_specs = (P(None, ("ctx", "head"), None), P("head", None, "ctx"))
    grid_rows = mesh.shape["ctx"] // ROWS
    return jax.shard_map(
        functools.partial(body, grid_rows),
        mesh=mesh,
        in_specs=in_specs,
        out_specs=out_specs,
        check_vma=False,
    )
```

time: 488 us -> 108 us (0.22)
  the two profiles are of different devices: /device:TPU:48 before, /device:TPU:56 now
where the time goes in v1:
time: 108 us
  starting transfers between devices  35.6 us (33%)
  waiting for transfers between devices  33.6 us (31%)
  blocking collectives  28.9 us (27%)
  Pallas kernels  4.39 us (4%)
  local copies, waits for them, and re-layouts  2.69 us (2%)
  other arithmetic  1.6 us (1%)
    ppermute x4, waiting for transfers between devices, shift(): return lax.ppermute(array, 'ctx', pairs)  33.6 us
    all_to_all x1, blocking collectives, body(): lax.all_to_all(blocks, 'head', split_axis=0, concat_axis=0, tiled=True)  28.9 us
    all_to_all x2, starting transfers between devices, row_gather(): lax.all_to_all(sent, 'ctx', split_axis=0, concat_axis=0, tiled=True, axis...  18.7 us
    ppermute x4, starting transfers between devices, shift(): return lax.ppermute(array, 'ctx', pairs)  16.9 us
    pallas_call x1, Pallas kernels, attend_rows(): pl.pallas_call(functools.partial(attention_kernel, 1.0 / head_dim ** 0.5,...  4.39 us
  transfers between devices with their start and end apart: 6, of which 3 were waited for; matrix products, arithmetic and copies ran while one was open for 0% of the time, Pallas kernels for 0%

profile of v1, /device:TPU:56, one launch (start us, length us, event | category | flops | bytes accessed | tf_op | source)
XLA Modules:
  0.0 107.6 jit_solution(4886393474560125630)
XLA Ops:
  0.6 0.7 convert_element_type.5
  1.3 0.9 fusion.1
  2.2 0.8 broadcast_in_dim.18
  3.1 10.3 %all-to-all-start = ((bf16[4,1,264,256]{3,2,1,0:T(8,128)(2,1)}), bf16[4,1,264,256]{3,2,1,0:T(8,128)(2,1)S(1)}, u32[]{:S(2)}, u32[]{:S(2)}) async-start(bf16[4,1,264,256]{3,2,1,0:T(8,128)(2,1)} %broadcast_in_dim.18), calls=%async_computation | async-start | bytes 1081344 | tf_op jit(solution)/shard_map/all_to_all | solution.py:167
  13.3 3.7 %collective-permute-start.2 = (bf16[1,264,256]{2,1,0:T(8,128)(2,1)S(1)}, bf16[1,264,256]{2,1,0:T(8,128)(2,1)S(1)}, u32[]{:S(2)}, u32[]{:S(2)}) collective-permute-start(bf16[1,264,256]{2,1,0:T(8,128)(2,1)S(1)} %get-tuple-element.7.own_ref), channel_id=1, source_target_pairs={{0,192},{16,208},{32,224},{48,240},{64,256},{80,272},{96,288},{112... | collective-permute-start | bytes 405512 | tf_op jit(solution)/shard_map/ppermute | solution.py:161
  17.0 5.9 %collective-permute-start.3 = (bf16[1,264,256]{2,1,0:T(8,128)(2,1)S(1)}, bf16[1,264,256]{2,1,0:T(8,128)(2,1)S(1)}, u32[]{:S(2)}, u32[]{:S(2)}) collective-permute-start(bf16[1,264,256]{2,1,0:T(8,128)(2,1)S(1)} %get-tuple-element.7.own_ref), channel_id=1, source_target_pairs={{0,256},{16,272},{32,288},{48,304},{64,320},{80,336},{96,352},{112... | collective-permute-start | bytes 405512 | tf_op jit(solution)/shard_map/ppermute | solution.py:161
  23.0 5.2 %collective-permute-done.2 = bf16[1,264,256]{2,1,0:T(8,128)(2,1)S(1)} collective-permute-done((bf16[1,264,256]{2,1,0:T(8,128)(2,1)S(1)}, bf16[1,264,256]{2,1,0:T(8,128)(2,1)S(1)}, u32[]{:S(2)}, u32[]{:S(2)}) %collective-permute-start.2) | collective-permute-done | bytes 135200 | tf_op jit(solution)/shard_map/ppermute | solution.py:161
  28.2 0.0 collective-permute-done.3
  28.2 0.0 all-to-all-done
  28.2 1.1 broadcast_in_dim.19
  29.3 0.0 copy-start
  29.3 0.0 copy-start.1
  29.3 8.4 %all-to-all-start.1 = ((bf16[4,2,264,256]{3,2,1,0:T(8,128)(2,1)}), bf16[4,2,264,256]{3,2,1,0:T(8,128)(2,1)S(1)}, u32[]{:S(2)}, u32[]{:S(2)}) async-start(bf16[4,2,264,256]{3,2,1,0:T(8,128)(2,1)} %broadcast_in_dim.19), calls=%async_computation.1 | async-start | bytes 2162688 | tf_op jit(solution)/shard_map/all_to_all | solution.py:167
  37.7 5.4 %collective-permute-start = (bf16[4,264,256]{2,1,0:T(8,128)(2,1)S(1)}, bf16[4,264,256]{2,1,0:T(8,128)(2,1)S(1)}, u32[]{:S(2)}, u32[]{:S(2)}) collective-permute-start(bf16[4,264,256]{2,1,0:T(8,128)(2,1)S(1)} %bitcast.10), channel_id=1, source_target_pairs={{0,64},{16,80},{32,96},{48,112},{64,128},{80,144},{96,160},{112,17... | collective-permute-start | bytes 1622024 | tf_op jit(solution)/shard_map/ppermute | solution.py:161
  43.1 15.4 %collective-permute-done.near1_hbm = bf16[4,264,256]{2,1,0:T(8,128)(2,1)S(1)} collective-permute-done((bf16[4,264,256]{2,1,0:T(8,128)(2,1)S(1)}, bf16[4,264,256]{2,1,0:T(8,128)(2,1)S(1)}, u32[]{:S(2)}, u32[]{:S(2)}) %collective-permute-start) | collective-permute-done | bytes 540704 | tf_op jit(solution)/shard_map/ppermute | solution.py:161
  58.5 1.9 %collective-permute-start.1 = (bf16[4,264,256]{2,1,0:T(8,128)(2,1)S(1)}, bf16[4,264,256]{2,1,0:T(8,128)(2,1)S(1)}, u32[]{:S(2)}, u32[]{:S(2)}) collective-permute-start(bf16[4,264,256]{2,1,0:T(8,128)(2,1)S(1)} %collective-permute-done.near1_hbm), channel_id=1, source_target_pairs={{0,64},{16,80},{32,96},{48,112},{64,128},{80,144},{96,160},{112,17... | collective-permute-start | bytes 1622024 | tf_op jit(solution)/shard_map/ppermute | solution.py:161
  60.4 0.0 all-to-all-done.1
  60.4 13.0 %collective-permute-done.1.near2_hbm = bf16[4,264,256]{2,1,0:T(8,128)(2,1)S(1)} collective-permute-done((bf16[4,264,256]{2,1,0:T(8,128)(2,1)S(1)}, bf16[4,264,256]{2,1,0:T(8,128)(2,1)S(1)}, u32[]{:S(2)}, u32[]{:S(2)}) %collective-permute-start.1) | collective-permute-done | bytes 540704 | tf_op jit(solution)/shard_map/ppermute | solution.py:161
  73.4 0.0 copy-done
  73.4 0.0 copy-done.1
  73.4 4.4 %attention.1 = (bf16[256,1024]{1,0:T(8,128)(2,1)S(1)}, f32[8,256]{1,0:T(8,128)}) custom-call(bf16[256,1024]{1,0:T(8,128)(2,1)S(1)} %bitcast.13, s32[1,256]{1,0:T(1,128)S(1)} %copy-done, bf16[1,264,256]{2,1,0:T(8,128)(2,1)S(1)} %get-tuple-element.7.own_ref, bf16[4,264,256]{2,1,0:T(8,128)(2,1)S(1)} %bitcast.11, ...), custom_call_target="tpu_custom_call" | custom-call | flops 5368709120 | bytes 4194304 | tf_op jit(solution)/shard_map/attention/pallas_call | solution.py:134
  77.8 28.9 %all_to_all.15 = bf16[16,16,1024]{2,1,0:T(8,128)(2,1)S(1)} all-to-all(bf16[16,16,1024]{2,1,0:T(8,128)(2,1)S(1)} %bitcast.12), channel_id=1, replica_groups=mesh['ctx'=32,'head'=16] {'head'}, dimensions={0} | all-to-all | bytes 1048576 | tf_op jit(solution)/shard_map/all_to_all | solution.py:185
  106.8 0.8 copy.7
  (1 shorter events, 0.0 us)
Async XLA Ops:
  3.1 25.2 %all-to-all-start = ((bf16[4,1,264,256]{3,2,1,0:T(8,128)(2,1)}), bf16[4,1,264,256]{3,2,1,0:T(8,128)(2,1)S(1)}, u32[]{:S(2)}, u32[]{:S(2)}) async-start(bf16[4,1,264,256]{3,2,1,0:T(8,128)(2,1)} %broadcast_in_dim.18), calls=%async_computation | async-start | bytes 1081344 | tf_op jit(solution)/shard_map/all_to_all | solution.py:167
  13.3 14.8 %collective-permute-start.2 = (bf16[1,264,256]{2,1,0:T(8,128)(2,1)S(1)}, bf16[1,264,256]{2,1,0:T(8,128)(2,1)S(1)}, u32[]{:S(2)}, u32[]{:S(2)}) collective-permute-start(bf16[1,264,256]{2,1,0:T(8,128)(2,1)S(1)} %get-tuple-element.7.own_ref), channel_id=1, source_target_pairs={{0,192},{16,208},{32,224},{48,240},{64,256},{80,272},{96,288},{112... | collective-permute-start | bytes 405512 | tf_op jit(solution)/shard_map/ppermute | solution.py:161
  17.0 11.2 %collective-permute-start.3 = (bf16[1,264,256]{2,1,0:T(8,128)(2,1)S(1)}, bf16[1,264,256]{2,1,0:T(8,128)(2,1)S(1)}, u32[]{:S(2)}, u32[]{:S(2)}) collective-permute-start(bf16[1,264,256]{2,1,0:T(8,128)(2,1)S(1)} %get-tuple-element.7.own_ref), channel_id=1, source_target_pairs={{0,256},{16,272},{32,288},{48,304},{64,320},{80,336},{96,352},{112... | collective-permute-start | bytes 405512 | tf_op jit(solution)/shard_map/ppermute | solution.py:161
  29.3 44.1 %copy-start = (s32[1,256]{1,0:T(1,128)S(1)}, s32[1,256]{1,0:T(1,128)}, u32[]{:S(2)}) copy-start(s32[1,256]{1,0:T(1,128)} %doc_ref.1) | copy-start | bytes 3076
  29.3 44.1 %copy-start.1 = (bf16[1,256,1024]{2,1,0:T(8,128)(2,1)S(1)}, bf16[1,256,1024]{2,1,0:T(8,128)(2,1)}, u32[]{:S(2)}) copy-start(bf16[1,256,1024]{2,1,0:T(8,128)(2,1)} %param.4) | copy-start | bytes 1572868
  29.3 31.1 %all-to-all-start.1 = ((bf16[4,2,264,256]{3,2,1,0:T(8,128)(2,1)}), bf16[4,2,264,256]{3,2,1,0:T(8,128)(2,1)S(1)}, u32[]{:S(2)}, u32[]{:S(2)}) async-start(bf16[4,2,264,256]{3,2,1,0:T(8,128)(2,1)} %broadcast_in_dim.19), calls=%async_computation.1 | async-start | bytes 2162688 | tf_op jit(solution)/shard_map/all_to_all | solution.py:167
  37.7 20.8 %collective-permute-start = (bf16[4,264,256]{2,1,0:T(8,128)(2,1)S(1)}, bf16[4,264,256]{2,1,0:T(8,128)(2,1)S(1)}, u32[]{:S(2)}, u32[]{:S(2)}) collective-permute-start(bf16[4,264,256]{2,1,0:T(8,128)(2,1)S(1)} %bitcast.10), channel_id=1, source_target_pairs={{0,64},{16,80},{32,96},{48,112},{64,128},{80,144},{96,160},{112,17... | collective-permute-start | bytes 1622024 | tf_op jit(solution)/shard_map/ppermute | solution.py:161
  58.5 15.0 %collective-permute-start.1 = (bf16[4,264,256]{2,1,0:T(8,128)(2,1)S(1)}, bf16[4,264,256]{2,1,0:T(8,128)(2,1)S(1)}, u32[]{:S(2)}, u32[]{:S(2)}) collective-permute-start(bf16[4,264,256]{2,1,0:T(8,128)(2,1)S(1)} %collective-permute-done.near1_hbm), channel_id=1, source_target_pairs={{0,64},{16,80},{32,96},{48,112},{64,128},{80,144},{96,160},{112,17... | collective-permute-start | bytes 1622024 | tf_op jit(solution)/shard_map/ppermute | solution.py:161

commit v2 on v1

v2 whole, which is shorter than its diff:
```python
import functools

import jax
import jax.numpy as jnp
import numpy as np
from jax import lax
from jax.experimental import pallas as pl
from jax.experimental.pallas import tpu as pltpu
from jax.sharding import PartitionSpec as P

NEG_FILL = -1e30
ROWS = 4
EXTRA = 8
SPAN = 4


def attention_kernel(sides, backs, has_own, has_state, last, scale, groups, head_dim, *refs):
    refs = list(refs)
    q_ref, doc_ref = refs.pop(0), refs.pop(0)
    own_ref = refs.pop(0) if has_own else None
    sources = [refs.pop(0) for _ in range(max(at for at, _ in sides) + 1)]
    in_state = [refs.pop(0), refs.pop(0)] if has_state else None
    if last:
        out_ref, lse_ref = refs.pop(0), refs.pop(0)
    else:
        out_state = [refs.pop(0), refs.pop(0)]
    buf, key_docs, flags = refs.pop(0), refs.pop(0), refs.pop(0)
    run_max, run_acc = (refs.pop(0), refs.pop(0)) if last else out_state
    sems = refs.pop(0)

    shard = q_ref.shape[0]
    place = lax.axis_index("ctx")
    row = place // ROWS
    col = lax.rem(place, ROWS)
    factor = scale
    copies = []
    for index, (at, side) in enumerate(sides):
        source = sources[at] if side is None else sources[at].at[:, side]
        copies.append(
            pltpu.make_async_copy(source, buf.at[pl.ds(index * ROWS, ROWS)], sems.at[index])
        )
    if has_state:
        copies.append(pltpu.make_async_copy(in_state[0], run_max, sems.at[len(sides)]))
        copies.append(pltpu.make_async_copy(in_state[1], run_acc, sems.at[len(sides) + 1]))
    for copy in copies:
        copy.start()

    doc_row = doc_ref[...].astype(jnp.float32)
    query_docs = jnp.transpose(jnp.broadcast_to(doc_row, (128, shard)))
    first_doc = jnp.min(doc_row)
    last_doc = jnp.max(doc_row)

    def attend(keys, vals, lines, fresh, old):
        vals = jnp.concatenate([vals, jnp.ones_like(vals)], axis=1)
        tiles = keys.shape[0] // 128

        def score(g):
            return lax.dot_general(
                q_ref[:, g * head_dim : (g + 1) * head_dim],
                keys,
                (((1,), (1,)), ((), ())),
                preferred_element_type=jnp.float32,
            )

        ahead = score(0)
        for g in range(groups):
            scores = ahead
            if g + 1 < groups:
                ahead = score(g + 1)
            if lines:
                parts = []
                for j in range(tiles):
                    at = j * 128 % shard
                    keep = query_docs == lines[j * 128 // shard][:, at : at + 128]
                    if fresh:
                        key_at = lax.broadcasted_iota(jnp.int32, (shard, 128), 1) + j * 128
                        keep = keep & (key_at <= lax.broadcasted_iota(jnp.int32, (shard, 128), 0))
                    parts.append(jnp.where(keep, scores[:, j * 128 : (j + 1) * 128], NEG_FILL))
                scores = jnp.concatenate(parts, axis=1)
            top = jnp.max(scores, axis=1, keepdims=True)
            if fresh:
                new_max = jnp.broadcast_to(top, (shard, 128))
            else:
                old_max = old[0][g]
                new_max = jnp.maximum(old_max, top)
            parts = [
                jnp.exp((scores[:, j * 128 : (j + 1) * 128] - new_max) * factor).astype(jnp.bfloat16)
                for j in range(tiles)
            ]
            mixed = jnp.dot(
                jnp.concatenate(parts, axis=1), vals, preferred_element_type=jnp.float32
            )
            if fresh:
                run_acc[g] = mixed
            else:
                fade = jnp.exp((old_max - new_max) * factor)
                run_acc[g, :, :head_dim] = old[1][g, :, :head_dim] * fade + mixed[:, :head_dim]
                run_acc[g, :, head_dim:] = old[1][g, :, head_dim:] * fade + mixed[:, head_dim:]
            run_max[g] = new_max

    def attend_chunk(chunk, masked):
        slots = [SPAN * chunk + j for j in range(SPAN)]
        keys = jnp.concatenate([buf[slot, :shard, :head_dim] for slot in slots], axis=0)
        vals = jnp.concatenate([buf[slot, :shard, head_dim:] for slot in slots], axis=0)
        lines = [key_docs[slot, 0:1, :] for slot in slots] if masked else []
        attend(keys, vals, lines, False, (run_max, run_acc))

    if has_own:
        attend(own_ref[0, :shard, :head_dim], own_ref[0, :shard, head_dim:], [doc_row], True, None)

    chunks = len(backs) * ROWS // SPAN
    for copy in copies:
        copy.wait()
    lines = []
    for index, rows_back in enumerate(backs):
        for at in range(ROWS):
            slot = index * ROWS + at
            line = buf[slot, shard : shard + EXTRA, :].astype(jnp.float32)[0:1, :]
            line = jnp.where(row >= rows_back if rows_back else at < col, line, -1.0)
            key_docs[slot] = jnp.broadcast_to(line, (8, shard))
            lines.append(line)
    for chunk in range(chunks):
        own_lines = lines[SPAN * chunk : SPAN * chunk + SPAN]
        low = jnp.min(functools.reduce(jnp.minimum, own_lines))
        high = jnp.max(functools.reduce(jnp.maximum, own_lines))
        flags[chunk] = jnp.where(high >= first_doc, jnp.where(low == last_doc, 1, 2), 0)

    @pl.loop(0, chunks)
    def _(chunk):
        flag = flags[chunk]

        @pl.when(flag == 1)
        def _():
            attend_chunk(chunk, False)

        @pl.when(flag == 2)
        def _():
            attend_chunk(chunk, True)

    if last:
        lane = lax.broadcasted_iota(jnp.int32, (shard, 128), 1)
        sums = jnp.zeros((shard, 128), jnp.float32)
        for g in range(groups):
            total = run_acc[g, :, head_dim:]
            out_ref[:, g * head_dim : (g + 1) * head_dim] = (
                run_acc[g, :, :head_dim] / total
            ).astype(jnp.bfloat16)
            sums = jnp.where(lane == g, run_max[g] * scale + jnp.log(total), sums)
        lse_ref[...] = jnp.transpose(sums)[:groups, :]


def attend_rows(queries, docs, own, state, arrays, sides, backs, last, weight=1):
    shard, width = queries.shape
    head_dim = arrays[0].shape[-1] // 2
    groups = width // head_dim
    anywhere = pl.BlockSpec(memory_space=pl.ANY)
    vmem = pl.BlockSpec(memory_space=pltpu.VMEM)
    state_shapes = [
        jax.ShapeDtypeStruct((groups, shard, 128), jnp.float32),
        jax.ShapeDtypeStruct((groups, shard, 2 * head_dim), jnp.float32),
    ]
    result = [
        jax.ShapeDtypeStruct((shard, width), jnp.bfloat16),
        jax.ShapeDtypeStruct((groups, shard), jnp.float32),
    ]
    slots = ROWS * len(sides)
    args = [queries, docs] + ([own] if own is not None else []) + list(arrays) + list(state or [])
    starts = len(args) - len(arrays) - len(state or [])
    specs = [vmem] * starts + [anywhere] * (len(args) - starts)
    scratch = [
        pltpu.VMEM((slots, shard + EXTRA, 2 * head_dim), jnp.bfloat16),
        pltpu.VMEM((slots, 8, shard), jnp.float32),
        pltpu.SMEM((slots // SPAN,), jnp.int32),
    ]
    if last:
        scratch += [pltpu.VMEM(s.shape, s.dtype) for s in state_shapes]
    scratch.append(pltpu.SemaphoreType.DMA((len(sides) + 2,)))
    work = shard * width * (slots + (own is not None)) * shard
    return pl.pallas_call(
        functools.partial(
            attention_kernel, tuple(sides), tuple(backs), own is not None, state is not None, last,
            1.0 / head_dim**0.5, groups, head_dim,
        ),
        out_shape=tuple(result if last else state_shapes),
        in_specs=specs,
        out_specs=(vmem, vmem),
        scratch_shapes=scratch,
        compiler_params=pltpu.CompilerParams(vmem_limit_bytes=16 << 20),
        cost_estimate=pl.CostEstimate(
            flops=4 * work * weight, bytes_accessed=4 << 20, transcendentals=work // head_dim
        ),
        name="attention",
    )(*args)

def shift(array, rows_on, grid_rows):
    count = grid_rows * ROWS
    pairs = [(place, (place + rows_on * ROWS) % count) for place in range(count)]
    return lax.ppermute(array, "ctx", pairs)


def row_gather(array, grid_rows):
    groups = [[r * ROWS + c for c in range(ROWS)] for r in range(grid_rows)]
    sent = jnp.broadcast_to(array[None], (ROWS, *array.shape))
    return lax.all_to_all(sent, "ctx", split_axis=0, concat_axis=0, tiled=True, axis_index_groups=groups)


def spread_kernel(first_ref, second_ref, after_ref, out_ref):
    for at in range(ROWS):
        out_ref[at, 0] = first_ref[...]
        out_ref[at, 1] = second_ref[...]


def spread(first, second, after):
    vmem = pl.BlockSpec(memory_space=pltpu.VMEM)
    return pl.pallas_call(
        spread_kernel,
        out_shape=jax.ShapeDtypeStruct((ROWS, 2, *first.shape), first.dtype),
        in_specs=[vmem, vmem, pl.BlockSpec(memory_space=pl.ANY)],
        out_specs=vmem,
        cost_estimate=pl.CostEstimate(flops=100 * 10**9, bytes_accessed=4 << 20, transcendentals=0),
        name="spread",
    )(first, second, after)


def exchange(sent, grid_rows):
    groups = [[r * ROWS + c for c in range(ROWS)] for r in range(grid_rows)]
    return lax.all_to_all(sent, "ctx", split_axis=0, concat_axis=0, tiled=True, axis_index_groups=groups)


def pack(keys, values, documents):
    packed = jnp.concatenate([keys[0], values[0]], axis=1)
    doc_rows = jnp.pad(documents.astype(jnp.bfloat16), ((0, EXTRA - 1), (0, 0)))
    return jnp.concatenate([packed, doc_rows], axis=0)


def body(grid_rows, queries, keys, values, documents):
    packed = pack(keys, values, documents)
    row = row_gather(packed, grid_rows)
    far3 = shift(packed, 3, grid_rows)
    far4 = shift(packed, 4, grid_rows)
    near1 = shift(row, 1, grid_rows)
    state = attend_rows(queries[0], documents, packed[None], None, [row], [(0, None)], [0], False, 1)
    far = exchange(spread(far3, far4, row), grid_rows)
    near1, state = lax.optimization_barrier((near1, state))
    near2 = shift(near1, 1, grid_rows)
    state = attend_rows(queries[0], documents, None, state, [near1], [(0, None)], [1], False, 1000)
    state = attend_rows(queries[0], documents, None, state, [near2], [(0, None)], [2], False)
    out, lse = attend_rows(queries[0], documents, None, state, [far], [(0, 0), (0, 1)], [3, 4], True)
    parts = lax.axis_size("head")
    blocks = out.reshape(parts, out.shape[0] // parts, out.shape[1])
    tokens = lax.all_to_all(blocks, "head", split_axis=0, concat_axis=0, tiled=True)
    return (tokens, lse[None])


def solution(mesh):
    in_specs = (
        P("head", "ctx", None),
        P("head", "ctx", None),
        P("head", "ctx", None),
        P("head", "ctx"),
    )
    out_specs = (P(None, ("ctx", "head"), None), P("head", None, "ctx"))
    grid_rows = mesh.shape["ctx"] // ROWS
    return jax.shard_map(
        functools.partial(body, grid_rows),
        mesh=mesh,
        in_specs=in_specs,
        out_specs=out_specs,
        check_vma=False,
    )
```

time: 108 us -> 97 us (0.90)
  the two profiles are of different devices: /device:TPU:56 before, /device:TPU:48 now
where the time goes in v2:
time: 97 us; the launch traced here: 95.5 us
  starting transfers between devices  31.5 us (32%)
  blocking collectives  25.3 us (26%)
  waiting for transfers between devices  20.2 us (21%)
  Pallas kernels  11.6 us (12%)
  local copies, waits for them, and re-layouts  4.52 us (5%)
  other arithmetic  1.58 us (2%)
    all_to_all x1, blocking collectives, body(): lax.all_to_all(blocks, 'head', split_axis=0, concat_axis=0, tiled=True)  25.3 us
    ppermute x4, starting transfers between devices, shift(): return lax.ppermute(array, 'ctx', pairs)  14.1 us
    ppermute x4, waiting for transfers between devices, shift(): return lax.ppermute(array, 'ctx', pairs)  13.6 us
    all_to_all x1, starting transfers between devices, row_gather(): lax.all_to_all(sent, 'ctx', split_axis=0, concat_axis=0, tiled=True, axis...  10.3 us
    pallas_call x4, Pallas kernels, attend_rows(): pl.pallas_call(functools.partial(attention_kernel, tuple(sides), tuple(ba...  9.6 us
    all_to_all x1, starting transfers between devices, exchange(): lax.all_to_all(sent, 'ctx', split_axis=0, concat_axis=0, tiled=True, axis...  7.08 us
    all_to_all x1, waiting for transfers between devices, row_gather(): lax.all_to_all(sent, 'ctx', split_axis=0, concat_axis=0, tiled=True, axis...  5.15 us
    unnamed x13, local copies, waits for them, and re-layouts  3.68 us
  transfers between devices with their start and end apart: 6, of which 4 were waited for; matrix products, arithmetic and copies ran while one was open for 0% of the time, Pallas kernels for 10%

profile of v2, /device:TPU:48, one launch (start us, length us, event | category | flops | bytes accessed | tf_op | source)
XLA Modules:
  0.0 95.5 jit_solution(6776664587971954021)
XLA Ops:
  0.6 0.7 convert_element_type.5
  1.3 0.9 fusion.2
  2.2 0.8 broadcast_in_dim.12
  3.1 10.3 %all-to-all-start = ((bf16[4,264,256]{2,1,0:T(8,128)(2,1)}), bf16[4,264,256]{2,1,0:T(8,128)(2,1)}, u32[]{:S(2)}, u32[]{:S(2)}) async-start(bf16[4,264,256]{2,1,0:T(8,128)(2,1)} %broadcast_in_dim.12), calls=%async_computation | async-start | bytes 1081344 | tf_op jit(solution)/shard_map/all_to_all | solution.py:204
  13.3 2.8 %collective-permute-start = (bf16[264,256]{1,0:T(8,128)(2,1)S(1)}, bf16[264,256]{1,0:T(8,128)(2,1)S(1)}, u32[]{:S(2)}, u32[]{:S(2)}) collective-permute-start(bf16[264,256]{1,0:T(8,128)(2,1)S(1)} %get-tuple-element.25), channel_id=1, source_target_pairs={{0,192},{16,208},{32,224},{48,240},{64,256},{80,272},{96,288},{112... | collective-permute-start | bytes 405512 | tf_op jit(solution)/shard_map/ppermute | solution.py:198
  16.1 6.8 %collective-permute-start.1 = (bf16[264,256]{1,0:T(8,128)(2,1)S(1)}, bf16[264,256]{1,0:T(8,128)(2,1)S(1)}, u32[]{:S(2)}, u32[]{:S(2)}) collective-permute-start(bf16[264,256]{1,0:T(8,128)(2,1)S(1)} %get-tuple-element.25), channel_id=1, source_target_pairs={{0,256},{16,272},{32,288},{48,304},{64,320},{80,336},{96,352},{112... | collective-permute-start | bytes 405512 | tf_op jit(solution)/shard_map/ppermute | solution.py:198
  23.0 5.2 %all-to-all-done.after_ref.refs_3_ = bf16[4,264,256]{2,1,0:T(8,128)(2,1)} async-done(((bf16[4,264,256]{2,1,0:T(8,128)(2,1)}), bf16[4,264,256]{2,1,0:T(8,128)(2,1)}, u32[]{:S(2)}, u32[]{:S(2)}) %all-to-all-start) | async-done | bytes 540704 | tf_op jit(solution)/shard_map/all_to_all | solution.py:204
  28.1 2.6 %collective-permute-start.2 = (bf16[4,264,256]{2,1,0:T(8,128)(2,1)}, bf16[4,264,256]{2,1,0:T(8,128)(2,1)}, u32[]{:S(2)}, u32[]{:S(2)}) collective-permute-start(bf16[4,264,256]{2,1,0:T(8,128)(2,1)} %all-to-all-done.after_ref.refs_3_), channel_id=1, source_target_pairs={{0,64},{16,80},{32,96},{48,112},{64,128},{80,144},{96,160},{112,17... | collective-permute-start | bytes 1622024 | tf_op jit(solution)/shard_map/ppermute | solution.py:198
  30.7 0.0 collective-permute-done.first_ref
  30.7 0.0 copy-start.4
  30.7 4.7 %collective-permute-done.1.second_ref = bf16[264,256]{1,0:T(8,128)(2,1)S(1)} collective-permute-done((bf16[264,256]{1,0:T(8,128)(2,1)S(1)}, bf16[264,256]{1,0:T(8,128)(2,1)S(1)}, u32[]{:S(2)}, u32[]{:S(2)}) %collective-permute-start.1) | collective-permute-done | bytes 135200 | tf_op jit(solution)/shard_map/ppermute | solution.py:198
  35.4 0.0 copy-done.4
  35.4 0.0 copy-start.5
  35.4 0.7 copy-done.5
  36.1 2.0 %spread.1 = bf16[4,2,264,256]{3,2,1,0:T(8,128)(2,1)} custom-call(bf16[264,256]{1,0:T(8,128)(2,1)} %copy-done.4, bf16[264,256]{1,0:T(8,128)(2,1)} %copy-done.5, bf16[4,264,256]{2,1,0:T(8,128)(2,1)} %all-to-all-done.after_ref.refs_3_), custom_call_target="tpu_custom_call" | custom-call | flops 99999997952 | bytes 4194304 | tf_op jit(solution)/shard_map/spread/pallas_call | solution.py:215
  38.1 0.0 copy-start
  38.1 0.0 copy-start.1
  38.1 7.1 %all-to-all-start.1 = ((bf16[4,2,264,256]{3,2,1,0:T(8,128)(2,1)}), bf16[4,2,264,256]{3,2,1,0:T(8,128)(2,1)}, u32[]{:S(2)}, u32[]{:S(2)}) async-start(bf16[4,2,264,256]{3,2,1,0:T(8,128)(2,1)} %spread.1), calls=%async_computation.1 | async-start | bytes 2162688 | tf_op jit(solution)/shard_map/all_to_all | solution.py:227
  45.2 0.0 copy-done
  45.2 0.0 copy-done.1
  45.2 1.2 %attention.4 = (f32[8,256,128]{2,1,0:T(8,128)S(1)}, f32[8,256,256]{2,1,0:T(8,128)S(1)}) custom-call(bf16[256,1024]{1,0:T(8,128)(2,1)S(1)} %bitcast.7, s32[1,256]{1,0:T(1,128)S(1)} %copy-done.1, bf16[1,264,256]{2,1,0:T(8,128)(2,1)S(1)} %get-tuple-element.24.refs_2_, bf16[4,264,256]{2,1,0:T(8,128)(2,1)} %all-to-all-done.after_ref.refs_3_), custom_call_target="tpu_custom_call" | custom-call | flops 1342177280 | bytes 4194304 | tf_op jit(solution)/shard_map/attention/pallas_call | solution.py:179
  46.4 0.0 collective-permute-done.2.refs_2_
  46.4 1.9 %collective-permute-start.3 = (bf16[4,264,256]{2,1,0:T(8,128)(2,1)}, bf16[4,264,256]{2,1,0:T(8,128)(2,1)}, u32[]{:S(2)}, u32[]{:S(2)}) collective-permute-start(bf16[4,264,256]{2,1,0:T(8,128)(2,1)} %collective-permute-done.2.refs_2_), channel_id=1, source_target_pairs={{0,64},{16,80},{32,96},{48,112},{64,128},{80,144},{96,160},{112,17... | collective-permute-start | bytes 1622024 | tf_op jit(solution)/shard_map/ppermute | solution.py:198
  48.4 4.7 %attention.5 = (f32[8,256,128]{2,1,0:T(8,128)S(1)}, f32[8,256,256]{2,1,0:T(8,128)S(1)}) custom-call(bf16[256,1024]{1,0:T(8,128)(2,1)S(1)} %bitcast.8, s32[1,256]{1,0:T(1,128)S(1)} %copy-done.1, bf16[4,264,256]{2,1,0:T(8,128)(2,1)} %collective-permute-done.2.refs_2_, f32[8,256,128]{2,1,0:T(8,128)S(1)} %get-tuple-element.16.refs_3_, ...), custom_call_target="tpu_custom_call" | custom-call | flops 1073741824000 | bytes 4194304 | tf_op jit(solution)/shard_map/attention/pallas_call | solution.py:179
  53.1 8.9 %collective-permute-done.3.refs_2_ = bf16[4,264,256]{2,1,0:T(8,128)(2,1)} collective-permute-done((bf16[4,264,256]{2,1,0:T(8,128)(2,1)}, bf16[4,264,256]{2,1,0:T(8,128)(2,1)}, u32[]{:S(2)}, u32[]{:S(2)}) %collective-permute-start.3) | collective-permute-done | bytes 540704 | tf_op jit(solution)/shard_map/ppermute | solution.py:198
  62.0 1.4 %attention.6 = (f32[8,256,128]{2,1,0:T(8,128)S(1)}, f32[8,256,256]{2,1,0:T(8,128)S(1)}) custom-call(bf16[256,1024]{1,0:T(8,128)(2,1)S(1)} %bitcast.9, s32[1,256]{1,0:T(1,128)S(1)} %copy-done.1, bf16[4,264,256]{2,1,0:T(8,128)(2,1)} %collective-permute-done.3.refs_2_, f32[8,256,128]{2,1,0:T(8,128)S(1)} %get-tuple-element.18.refs_3_, ...), custom_call_target="tpu_custom_call" | custom-call | flops 1073741824 | bytes 4194304 | tf_op jit(solution)/shard_map/attention/pallas_call | solution.py:179
  63.4 0.0 copy-start.2
  63.5 1.0 %copy-done.2 = f32[8,256,128]{2,1,0:T(8,128)} copy-done((f32[8,256,128]{2,1,0:T(8,128)}, f32[8,256,128]{2,1,0:T(8,128)S(1)}, u32[]{:S(2)}) %copy-start.2) | copy-done | bytes 1048600
  64.4 1.5 %all-to-all-done.1.refs_2_ = bf16[4,2,264,256]{3,2,1,0:T(8,128)(2,1)} async-done(((bf16[4,2,264,256]{3,2,1,0:T(8,128)(2,1)}), bf16[4,2,264,256]{3,2,1,0:T(8,128)(2,1)}, u32[]{:S(2)}, u32[]{:S(2)}) %all-to-all-start.1) | async-done | bytes 1081376 | tf_op jit(solution)/shard_map/all_to_all | solution.py:227
  65.9 0.0 copy-start.3
  65.9 1.2 %copy-done.3 = f32[8,256,128]{2,1,0:T(8,128)S(1)} copy-done((f32[8,256,128]{2,1,0:T(8,128)S(1)}, f32[8,256,128]{2,1,0:T(8,128)}, u32[]{:S(2)}) %copy-start.3) | copy-done | bytes 1048600
  67.1 2.2 %attention.7 = (bf16[256,1024]{1,0:T(8,128)(2,1)S(1)}, f32[8,256]{1,0:T(8,128)}) custom-call(bf16[256,1024]{1,0:T(8,128)(2,1)S(1)} %bitcast.10, s32[1,256]{1,0:T(1,128)S(1)} %copy-done.1, bf16[4,2,264,256]{3,2,1,0:T(8,128)(2,1)} %all-to-all-done.1.refs_2_, f32[8,256,128]{2,1,0:T(8,128)S(1)} %copy-done.3, f32[8,256,256]{2,1,0:T(8,128)S(1)} %get-tuple-element.21.refs_4_), custom_call_target="tpu_custom_call" | custom-call | flops 2147483648 | bytes 4194304 | tf_op jit(solution)/shard_map/attention/pallas_call | solution.py:179
  69.3 25.3 %all_to_all.15 = bf16[16,16,1024]{2,1,0:T(8,128)(2,1)S(1)} all-to-all(bf16[16,16,1024]{2,1,0:T(8,128)(2,1)S(1)} %bitcast.11), channel_id=1, replica_groups=mesh['ctx'=32,'head'=16] {'head'}, dimensions={0} | all-to-all | bytes 1048576 | tf_op jit(solution)/shard_map/all_to_all | solution.py:251
  94.7 0.8 copy.7
Async XLA Ops:
  3.1 25.1 %all-to-all-start = ((bf16[4,264,256]{2,1,0:T(8,128)(2,1)}), bf16[4,264,256]{2,1,0:T(8,128)(2,1)}, u32[]{:S(2)}, u32[]{:S(2)}) async-start(bf16[4,264,256]{2,1,0:T(8,128)(2,1)} %broadcast_in_dim.12), calls=%async_computation | async-start | bytes 1081344 | tf_op jit(solution)/shard_map/all_to_all | solution.py:204
  13.3 17.4 %collective-permute-start = (bf16[264,256]{1,0:T(8,128)(2,1)S(1)}, bf16[264,256]{1,0:T(8,128)(2,1)S(1)}, u32[]{:S(2)}, u32[]{:S(2)}) collective-permute-start(bf16[264,256]{1,0:T(8,128)(2,1)S(1)} %get-tuple-element.25), channel_id=1, source_target_pairs={{0,192},{16,208},{32,224},{48,240},{64,256},{80,272},{96,288},{112... | collective-permute-start | bytes 405512 | tf_op jit(solution)/shard_map/ppermute | solution.py:198
  16.1 19.3 %collective-permute-start.1 = (bf16[264,256]{1,0:T(8,128)(2,1)S(1)}, bf16[264,256]{1,0:T(8,128)(2,1)S(1)}, u32[]{:S(2)}, u32[]{:S(2)}) collective-permute-start(bf16[264,256]{1,0:T(8,128)(2,1)S(1)} %get-tuple-element.25), channel_id=1, source_target_pairs={{0,256},{16,272},{32,288},{48,304},{64,320},{80,336},{96,352},{112... | collective-permute-start | bytes 405512 | tf_op jit(solution)/shard_map/ppermute | solution.py:198
  28.1 18.3 %collective-permute-start.2 = (bf16[4,264,256]{2,1,0:T(8,128)(2,1)}, bf16[4,264,256]{2,1,0:T(8,128)(2,1)}, u32[]{:S(2)}, u32[]{:S(2)}) collective-permute-start(bf16[4,264,256]{2,1,0:T(8,128)(2,1)} %all-to-all-done.after_ref.refs_3_), channel_id=1, source_target_pairs={{0,64},{16,80},{32,96},{48,112},{64,128},{80,144},{96,160},{112,17... | collective-permute-start | bytes 1622024 | tf_op jit(solution)/shard_map/ppermute | solution.py:198
  30.7 4.7 %copy-start.4 = (bf16[264,256]{1,0:T(8,128)(2,1)}, bf16[264,256]{1,0:T(8,128)(2,1)S(1)}, u32[]{:S(2)}) copy-start(bf16[264,256]{1,0:T(8,128)(2,1)S(1)} %collective-permute-done.first_ref) | copy-start | bytes 405508
  35.4 0.7 copy-start.5
  38.1 7.1 %copy-start = (bf16[1,256,1024]{2,1,0:T(8,128)(2,1)S(1)}, bf16[1,256,1024]{2,1,0:T(8,128)(2,1)}, u32[]{:S(2)}) copy-start(bf16[1,256,1024]{2,1,0:T(8,128)(2,1)} %param.4) | copy-start | bytes 1572868
  38.1 7.1 %copy-start.1 = (s32[1,256]{1,0:T(1,128)S(1)}, s32[1,256]{1,0:T(1,128)}, u32[]{:S(2)}) copy-start(s32[1,256]{1,0:T(1,128)} %refs_1_.7) | copy-start | bytes 3076
  38.1 27.8 %all-to-all-start.1 = ((bf16[4,2,264,256]{3,2,1,0:T(8,128)(2,1)}), bf16[4,2,264,256]{3,2,1,0:T(8,128)(2,1)}, u32[]{:S(2)}, u32[]{:S(2)}) async-start(bf16[4,2,264,256]{3,2,1,0:T(8,128)(2,1)} %spread.1), calls=%async_computation.1 | async-start | bytes 2162688 | tf_op jit(solution)/shard_map/all_to_all | solution.py:227
  46.4 15.6 %collective-permute-start.3 = (bf16[4,264,256]{2,1,0:T(8,128)(2,1)}, bf16[4,264,256]{2,1,0:T(8,128)(2,1)}, u32[]{:S(2)}, u32[]{:S(2)}) collective-permute-start(bf16[4,264,256]{2,1,0:T(8,128)(2,1)} %collective-permute-done.2.refs_2_), channel_id=1, source_target_pairs={{0,64},{16,80},{32,96},{48,112},{64,128},{80,144},{96,160},{112,17... | collective-permute-start | bytes 1622024 | tf_op jit(solution)/shard_map/ppermute | solution.py:198
  63.4 1.0 %copy-start.2 = (f32[8,256,128]{2,1,0:T(8,128)}, f32[8,256,128]{2,1,0:T(8,128)S(1)}, u32[]{:S(2)}) copy-start(f32[8,256,128]{2,1,0:T(8,128)S(1)} %get-tuple-element.20.refs_3_) | copy-start | bytes 3145732
  65.9 1.2 %copy-start.3 = (f32[8,256,128]{2,1,0:T(8,128)S(1)}, f32[8,256,128]{2,1,0:T(8,128)}, u32[]{:S(2)}) copy-start(f32[8,256,128]{2,1,0:T(8,128)} %copy-done.2) | copy-start | bytes 3145732

commit v3 on v2

--- a/solution.py
+++ b/solution.py
@@ -198,12 +198,6 @@
     return lax.ppermute(array, "ctx", pairs)
 
 
-def row_gather(array, grid_rows):
-    groups = [[r * ROWS + c for c in range(ROWS)] for r in range(grid_rows)]
-    sent = jnp.broadcast_to(array[None], (ROWS, *array.shape))
-    return lax.all_to_all(sent, "ctx", split_axis=0, concat_axis=0, tiled=True, axis_index_groups=groups)
-
-
 def spread_kernel(first_ref, second_ref, after_ref, out_ref):
     for at in range(ROWS):
         out_ref[at, 0] = first_ref[...]
@@ -227,21 +221,41 @@
     return lax.all_to_all(sent, "ctx", split_axis=0, concat_axis=0, tiled=True, axis_index_groups=groups)
 
 
+def pack_kernel(key_ref, value_ref, doc_ref, packed_ref, sent_ref):
+    shard, head_dim = key_ref.shape
+    docs = doc_ref[...].astype(jnp.float32)
+    first = lax.broadcasted_iota(jnp.int32, (EXTRA, shard), 0) == 0
+    docs = jnp.where(first, docs, 0.0).astype(jnp.bfloat16)
+    for ref in [packed_ref.at[0]] + [sent_ref.at[at] for at in range(ROWS)]:
+        ref[:shard, :head_dim] = key_ref[...]
+        ref[:shard, head_dim:] = value_ref[...]
+        ref[shard:, :] = docs
+
+
 def pack(keys, values, documents):
-    packed = jnp.concatenate([keys[0], values[0]], axis=1)
-    doc_rows = jnp.pad(documents.astype(jnp.bfloat16), ((0, EXTRA - 1), (0, 0)))
-    return jnp.concatenate([packed, doc_rows], axis=0)
+    shard, head_dim = keys.shape
+    block = (shard + EXTRA, 2 * head_dim)
+    vmem = pl.BlockSpec(memory_space=pltpu.VMEM)
+    return pl.pallas_call(
+        pack_kernel,
+        out_shape=(
+            jax.ShapeDtypeStruct((1, *block), keys.dtype),
+            jax.ShapeDtypeStruct((ROWS, *block), keys.dtype),
+        ),
+        in_specs=[vmem] * 3,
+        out_specs=(vmem, vmem),
+        name="pack",
+    )(keys, values, documents)
 
 
 def body(grid_rows, queries, keys, values, documents):
-    packed = pack(keys, values, documents)
-    row = row_gather(packed, grid_rows)
+    packed, sent = pack(keys[0], values[0], documents)
+    row = exchange(sent, grid_rows)
     far3 = shift(packed, 3, grid_rows)
     far4 = shift(packed, 4, grid_rows)
     near1 = shift(row, 1, grid_rows)
-    state = attend_rows(queries[0], documents, packed[None], None, [row], [(0, None)], [0], False, 1)
-    far = exchange(spread(far3, far4, row), grid_rows)
-    near1, state = lax.optimization_barrier((near1, state))
+    state = attend_rows(queries[0], documents, packed, None, [row], [(0, None)], [0], False, 1)
+    far = exchange(spread(far3[0], far4[0], row), grid_rows)
     near2 = shift(near1, 1, grid_rows)
     state = attend_rows(queries[0], documents, None, state, [near1], [(0, None)], [1], False, 1000)
     state = attend_rows(queries[0], documents, None, state, [near2], [(0, None)], [2], False)

time: 97 us -> 98.8 us (1.019); the launches traced: 95.5 us -> 99.4 us
  blocking collectives: 25.3 us -> 29.7 us
  Pallas kernels: 11.6 us -> 13.4 us
  other arithmetic: 1.58 us -> 0 us
    all_to_all x1 -> x0, starting transfers between devices: 10.3 us -> none  [row_gather(): lax.all_to_all(sent, 'ctx', split_axis=0, concat_axis=0, tiled=True, axis...]
    all_to_all x1 -> x2, starting transfers between devices: 7.08 us -> 17.4 us  [exchange(): lax.all_to_all(sent, 'ctx', split_axis=0, concat_axis=0, tiled=True, axis...]
    all_to_all x1 -> x0, waiting for transfers between devices: 5.15 us -> none  [row_gather(): lax.all_to_all(sent, 'ctx', split_axis=0, concat_axis=0, tiled=True, axis...]
    all_to_all x1 -> x2, waiting for transfers between devices: 1.45 us -> 6.6 us  [exchange(): lax.all_to_all(sent, 'ctx', split_axis=0, concat_axis=0, tiled=True, axis...]
    all_to_all x1, blocking collectives: 25.3 us -> 29.7 us  [body(): lax.all_to_all(blocks, 'head', split_axis=0, concat_axis=0, tiled=True)]
    pallas_call x0 -> x1, Pallas kernels: none -> 1.79 us  [pack(): pl.pallas_call(pack_kernel, out_shape=(jax.ShapeDtypeStruct((1, *block),...]
    unnamed x13 -> x15, local copies, waits for them, and re-layouts: 3.68 us -> 3.65 us
  transfers between devices with their start and end apart: 6 -> 6, of which waited for: 4 -> 4; matrix products, arithmetic and copies ran while one was open for 0% -> 0% of each run, Pallas kernels for 10% -> 9%
where the time goes in v3:
time: 98.8 us; the launch traced here: 99.4 us
  starting transfers between devices  31.5 us (32%)
  blocking collectives  29.7 us (30%)
  waiting for transfers between devices  20.4 us (21%)
  Pallas kernels  13.4 us (14%)
  local copies, waits for them, and re-layouts  3.65 us (4%)
    all_to_all x1, blocking collectives, body(): lax.all_to_all(blocks, 'head', split_axis=0, concat_axis=0, tiled=True)  29.7 us
    all_to_all x2, starting transfers between devices, exchange(): lax.all_to_all(sent, 'ctx', split_axis=0, concat_axis=0, tiled=True, axis...  17.4 us
    ppermute x4, starting transfers between devices, shift(): return lax.ppermute(array, 'ctx', pairs)  14.1 us
    ppermute x4, waiting for transfers between devices, shift(): return lax.ppermute(array, 'ctx', pairs)  13.8 us
    pallas_call x4, Pallas kernels, attend_rows(): pl.pallas_call(functools.partial(attention_kernel, tuple(sides), tuple(ba...  9.6 us
    all_to_all x2, waiting for transfers between devices, exchange(): lax.all_to_all(sent, 'ctx', split_axis=0, concat_axis=0, tiled=True, axis...  6.6 us
    unnamed x15, local copies, waits for them, and re-layouts  3.65 us
    pallas_call x1, Pallas kernels, spread(): pl.pallas_call(spread_kernel, out_shape=jax.ShapeDtypeStruct((ROWS, 2, *f...  2.04 us
  transfers between devices with their start and end apart: 6, of which 4 were waited for; matrix products, arithmetic and copies ran while one was open for 0% of the time, Pallas kernels for 9%

profile of v3, /device:TPU:48, one launch (start us, length us, event | category | flops | bytes accessed | tf_op | source)
XLA Modules:
  0.0 99.4 jit_solution(5511599207999897467)
XLA Ops:
  0.6 1.8 %pack.1 = (bf16[1,264,256]{2,1,0:T(8,128)(2,1)}, bf16[4,264,256]{2,1,0:T(8,128)(2,1)}) custom-call(bf16[256,128]{1,0:T(8,128)(2,1)} %bitcast.12, bf16[256,128]{1,0:T(8,128)(2,1)} %bitcast.13, s32[1,256]{1,0:T(1,128)} %refs_1_.7), custom_call_target="tpu_custom_call" | custom-call | tf_op jit(solution)/shard_map/pack/pallas_call | solution.py:239
  2.4 10.3 %all-to-all-start = ((bf16[4,264,256]{2,1,0:T(8,128)(2,1)}), bf16[4,264,256]{2,1,0:T(8,128)(2,1)}, u32[]{:S(2)}, u32[]{:S(2)}) async-start(bf16[4,264,256]{2,1,0:T(8,128)(2,1)} %get-tuple-element.13), calls=%async_computation | async-start | bytes 1081344 | tf_op jit(solution)/shard_map/all_to_all | solution.py:221
  12.7 2.8 %collective-permute-start = (bf16[1,264,256]{2,1,0:T(8,128)(2,1)}, bf16[1,264,256]{2,1,0:T(8,128)(2,1)S(1)}, u32[]{:S(2)}, u32[]{:S(2)}) collective-permute-start(bf16[1,264,256]{2,1,0:T(8,128)(2,1)} %get-tuple-element.12.refs_2_), channel_id=1, source_target_pairs={{0,192},{16,208},{32,224},{48,240},{64,256},{80,272},{96,288},{112... | collective-permute-start | bytes 405512 | tf_op jit(solution)/shard_map/ppermute | solution.py:198
  15.5 6.8 %collective-permute-start.1 = (bf16[1,264,256]{2,1,0:T(8,128)(2,1)}, bf16[1,264,256]{2,1,0:T(8,128)(2,1)S(1)}, u32[]{:S(2)}, u32[]{:S(2)}) collective-permute-start(bf16[1,264,256]{2,1,0:T(8,128)(2,1)} %get-tuple-element.12.refs_2_), channel_id=1, source_target_pairs={{0,256},{16,272},{32,288},{48,304},{64,320},{80,336},{96,352},{112... | collective-permute-start | bytes 405512 | tf_op jit(solution)/shard_map/ppermute | solution.py:198
  22.4 5.2 %all-to-all-done.after_ref.refs_3_ = bf16[4,264,256]{2,1,0:T(8,128)(2,1)} async-done(((bf16[4,264,256]{2,1,0:T(8,128)(2,1)}), bf16[4,264,256]{2,1,0:T(8,128)(2,1)}, u32[]{:S(2)}, u32[]{:S(2)}) %all-to-all-start) | async-done | bytes 540704 | tf_op jit(solution)/shard_map/all_to_all | solution.py:221
  27.5 2.6 %collective-permute-start.2 = (bf16[4,264,256]{2,1,0:T(8,128)(2,1)}, bf16[4,264,256]{2,1,0:T(8,128)(2,1)}, u32[]{:S(2)}, u32[]{:S(2)}) collective-permute-start(bf16[4,264,256]{2,1,0:T(8,128)(2,1)} %all-to-all-done.after_ref.refs_3_), channel_id=1, source_target_pairs={{0,64},{16,80},{32,96},{48,112},{64,128},{80,144},{96,160},{112,17... | collective-permute-start | bytes 1622024 | tf_op jit(solution)/shard_map/ppermute | solution.py:198
  30.1 0.0 collective-permute-done
  30.1 0.0 copy-start.5
  30.1 4.9 %collective-permute-done.1 = bf16[1,264,256]{2,1,0:T(8,128)(2,1)S(1)} collective-permute-done((bf16[1,264,256]{2,1,0:T(8,128)(2,1)}, bf16[1,264,256]{2,1,0:T(8,128)(2,1)S(1)}, u32[]{:S(2)}, u32[]{:S(2)}) %collective-permute-start.1) | collective-permute-done | bytes 135200 | tf_op jit(solution)/shard_map/ppermute | solution.py:198
  35.0 0.0 copy-start.6
  35.0 0.0 copy-done.5
  35.0 0.6 copy-done.6
  35.6 2.0 %spread.1 = bf16[4,2,264,256]{3,2,1,0:T(8,128)(2,1)} custom-call(bf16[264,256]{1,0:T(8,128)(2,1)} %bitcast.14, bf16[264,256]{1,0:T(8,128)(2,1)} %bitcast.15, bf16[4,264,256]{2,1,0:T(8,128)(2,1)} %all-to-all-done.after_ref.refs_3_), custom_call_target="tpu_custom_call" | custom-call | flops 99999997952 | bytes 4194304 | tf_op jit(solution)/shard_map/spread/pallas_call | solution.py:209
  37.7 0.0 copy-start
  37.7 0.0 copy-start.1
  37.7 0.0 copy-start.4
  37.7 7.1 %all-to-all-start.1 = ((bf16[4,2,264,256]{3,2,1,0:T(8,128)(2,1)}), bf16[4,2,264,256]{3,2,1,0:T(8,128)(2,1)}, u32[]{:S(2)}, u32[]{:S(2)}) async-start(bf16[4,2,264,256]{3,2,1,0:T(8,128)(2,1)} %spread.1), calls=%async_computation.1 | async-start | bytes 2162688 | tf_op jit(solution)/shard_map/all_to_all | solution.py:221
  44.8 0.0 copy-done
  44.8 0.0 copy-done.1
  44.8 0.0 copy-done.4
  44.8 1.2 %attention.4 = (f32[8,256,128]{2,1,0:T(8,128)S(1)}, f32[8,256,256]{2,1,0:T(8,128)S(1)}) custom-call(bf16[256,1024]{1,0:T(8,128)(2,1)S(1)} %bitcast.7, s32[1,256]{1,0:T(1,128)S(1)} %copy-done.1, bf16[1,264,256]{2,1,0:T(8,128)(2,1)S(1)} %copy-done.4, bf16[4,264,256]{2,1,0:T(8,128)(2,1)} %all-to-all-done.after_ref.refs_3_), custom_call_target="tpu_custom_call" | custom-call | flops 1342177280 | bytes 4194304 | tf_op jit(solution)/shard_map/attention/pallas_call | solution.py:179
  46.0 0.0 collective-permute-done.2.refs_2_
  46.0 1.9 %collective-permute-start.3 = (bf16[4,264,256]{2,1,0:T(8,128)(2,1)}, bf16[4,264,256]{2,1,0:T(8,128)(2,1)}, u32[]{:S(2)}, u32[]{:S(2)}) collective-permute-start(bf16[4,264,256]{2,1,0:T(8,128)(2,1)} %collective-permute-done.2.refs_2_), channel_id=1, source_target_pairs={{0,64},{16,80},{32,96},{48,112},{64,128},{80,144},{96,160},{112,17... | collective-permute-start | bytes 1622024 | tf_op jit(solution)/shard_map/ppermute | solution.py:198
  47.9 4.7 %attention.5 = (f32[8,256,128]{2,1,0:T(8,128)S(1)}, f32[8,256,256]{2,1,0:T(8,128)S(1)}) custom-call(bf16[256,1024]{1,0:T(8,128)(2,1)S(1)} %bitcast.8, s32[1,256]{1,0:T(1,128)S(1)} %copy-done.1, bf16[4,264,256]{2,1,0:T(8,128)(2,1)} %collective-permute-done.2.refs_2_, f32[8,256,128]{2,1,0:T(8,128)S(1)} %get-tuple-element.14.refs_3_, ...), custom_call_target="tpu_custom_call" | custom-call | flops 1073741824000 | bytes 4194304 | tf_op jit(solution)/shard_map/attention/pallas_call | solution.py:179
  52.7 8.9 %collective-permute-done.3.refs_2_ = bf16[4,264,256]{2,1,0:T(8,128)(2,1)} collective-permute-done((bf16[4,264,256]{2,1,0:T(8,128)(2,1)}, bf16[4,264,256]{2,1,0:T(8,128)(2,1)}, u32[]{:S(2)}, u32[]{:S(2)}) %collective-permute-start.3) | collective-permute-done | bytes 540704 | tf_op jit(solution)/shard_map/ppermute | solution.py:198
  61.6 1.4 %attention.6 = (f32[8,256,128]{2,1,0:T(8,128)S(1)}, f32[8,256,256]{2,1,0:T(8,128)S(1)}) custom-call(bf16[256,1024]{1,0:T(8,128)(2,1)S(1)} %bitcast.9, s32[1,256]{1,0:T(1,128)S(1)} %copy-done.1, bf16[4,264,256]{2,1,0:T(8,128)(2,1)} %collective-permute-done.3.refs_2_, f32[8,256,128]{2,1,0:T(8,128)S(1)} %get-tuple-element.16.refs_3_, ...), custom_call_target="tpu_custom_call" | custom-call | flops 1073741824 | bytes 4194304 | tf_op jit(solution)/shard_map/attention/pallas_call | solution.py:179
  63.0 0.0 copy-start.2
  63.0 1.0 copy-done.2
  64.0 1.4 %all-to-all-done.1.refs_2_ = bf16[4,2,264,256]{3,2,1,0:T(8,128)(2,1)} async-done(((bf16[4,2,264,256]{3,2,1,0:T(8,128)(2,1)}), bf16[4,2,264,256]{3,2,1,0:T(8,128)(2,1)}, u32[]{:S(2)}, u32[]{:S(2)}) %all-to-all-start.1) | async-done | bytes 1081376 | tf_op jit(solution)/shard_map/all_to_all | solution.py:221
  65.5 0.0 copy-start.3
  65.5 1.2 %copy-done.3 = f32[8,256,128]{2,1,0:T(8,128)S(1)} copy-done((f32[8,256,128]{2,1,0:T(8,128)S(1)}, f32[8,256,128]{2,1,0:T(8,128)}, u32[]{:S(2)}) %copy-start.3) | copy-done | bytes 1048600
  66.7 2.2 %attention.7 = (bf16[256,1024]{1,0:T(8,128)(2,1)S(1)}, f32[8,256]{1,0:T(8,128)}) custom-call(bf16[256,1024]{1,0:T(8,128)(2,1)S(1)} %bitcast.10, s32[1,256]{1,0:T(1,128)S(1)} %copy-done.1, bf16[4,2,264,256]{3,2,1,0:T(8,128)(2,1)} %all-to-all-done.1.refs_2_, f32[8,256,128]{2,1,0:T(8,128)S(1)} %copy-done.3, f32[8,256,256]{2,1,0:T(8,128)S(1)} %get-tuple-element.19.refs_4_), custom_call_target="tpu_custom_call" | custom-call | flops 2147483648 | bytes 4194304 | tf_op jit(solution)/shard_map/attention/pallas_call | solution.py:179
  68.9 29.7 %all_to_all.15 = bf16[16,16,1024]{2,1,0:T(8,128)(2,1)S(1)} all-to-all(bf16[16,16,1024]{2,1,0:T(8,128)(2,1)S(1)} %bitcast.11), channel_id=1, replica_groups=mesh['ctx'=32,'head'=16] {'head'}, dimensions={0} | all-to-all | bytes 1048576 | tf_op jit(solution)/shard_map/all_to_all | solution.py:265
  98.6 0.8 copy.7
Async XLA Ops:
  2.4 25.1 %all-to-all-start = ((bf16[4,264,256]{2,1,0:T(8,128)(2,1)}), bf16[4,264,256]{2,1,0:T(8,128)(2,1)}, u32[]{:S(2)}, u32[]{:S(2)}) async-start(bf16[4,264,256]{2,1,0:T(8,128)(2,1)} %get-tuple-element.13), calls=%async_computation | async-start | bytes 1081344 | tf_op jit(solution)/shard_map/all_to_all | solution.py:221
  12.7 17.4 %collective-permute-start = (bf16[1,264,256]{2,1,0:T(8,128)(2,1)}, bf16[1,264,256]{2,1,0:T(8,128)(2,1)S(1)}, u32[]{:S(2)}, u32[]{:S(2)}) collective-permute-start(bf16[1,264,256]{2,1,0:T(8,128)(2,1)} %get-tuple-element.12.refs_2_), channel_id=1, source_target_pairs={{0,192},{16,208},{32,224},{48,240},{64,256},{80,272},{96,288},{112... | collective-permute-start | bytes 405512 | tf_op jit(solution)/shard_map/ppermute | solution.py:198
  15.5 19.5 %collective-permute-start.1 = (bf16[1,264,256]{2,1,0:T(8,128)(2,1)}, bf16[1,264,256]{2,1,0:T(8,128)(2,1)S(1)}, u32[]{:S(2)}, u32[]{:S(2)}) collective-permute-start(bf16[1,264,256]{2,1,0:T(8,128)(2,1)} %get-tuple-element.12.refs_2_), channel_id=1, source_target_pairs={{0,256},{16,272},{32,288},{48,304},{64,320},{80,336},{96,352},{112... | collective-permute-start | bytes 405512 | tf_op jit(solution)/shard_map/ppermute | solution.py:198
  27.5 18.5 %collective-permute-start.2 = (bf16[4,264,256]{2,1,0:T(8,128)(2,1)}, bf16[4,264,256]{2,1,0:T(8,128)(2,1)}, u32[]{:S(2)}, u32[]{:S(2)}) collective-permute-start(bf16[4,264,256]{2,1,0:T(8,128)(2,1)} %all-to-all-done.after_ref.refs_3_), channel_id=1, source_target_pairs={{0,64},{16,80},{32,96},{48,112},{64,128},{80,144},{96,160},{112,17... | collective-permute-start | bytes 1622024 | tf_op jit(solution)/shard_map/ppermute | solution.py:198
  30.1 4.9 %copy-start.5 = (bf16[1,264,256]{2,1,0:T(8,128)(2,1)}, bf16[1,264,256]{2,1,0:T(8,128)(2,1)S(1)}, u32[]{:S(2)}) copy-start(bf16[1,264,256]{2,1,0:T(8,128)(2,1)S(1)} %collective-permute-done) | copy-start | bytes 405508
  35.0 0.7 copy-start.6
  37.7 7.1 %copy-start = (bf16[1,256,1024]{2,1,0:T(8,128)(2,1)S(1)}, bf16[1,256,1024]{2,1,0:T(8,128)(2,1)}, u32[]{:S(2)}) copy-start(bf16[1,256,1024]{2,1,0:T(8,128)(2,1)} %param.4) | copy-start | bytes 1572868
  37.7 7.1 %copy-start.1 = (s32[1,256]{1,0:T(1,128)S(1)}, s32[1,256]{1,0:T(1,128)}, u32[]{:S(2)}) copy-start(s32[1,256]{1,0:T(1,128)} %refs_1_.7) | copy-start | bytes 3076
  37.7 7.1 %copy-start.4 = (bf16[1,264,256]{2,1,0:T(8,128)(2,1)S(1)}, bf16[1,264,256]{2,1,0:T(8,128)(2,1)}, u32[]{:S(2)}) copy-start(bf16[1,264,256]{2,1,0:T(8,128)(2,1)} %get-tuple-element.12.refs_2_) | copy-start | bytes 405508
  37.7 27.8 %all-to-all-start.1 = ((bf16[4,2,264,256]{3,2,1,0:T(8,128)(2,1)}), bf16[4,2,264,256]{3,2,1,0:T(8,128)(2,1)}, u32[]{:S(2)}, u32[]{:S(2)}) async-start(bf16[4,2,264,256]{3,2,1,0:T(8,128)(2,1)} %spread.1), calls=%async_computation.1 | async-start | bytes 2162688 | tf_op jit(solution)/shard_map/all_to_all | solution.py:221
  46.0 15.6 %collective-permute-start.3 = (bf16[4,264,256]{2,1,0:T(8,128)(2,1)}, bf16[4,264,256]{2,1,0:T(8,128)(2,1)}, u32[]{:S(2)}, u32[]{:S(2)}) collective-permute-start(bf16[4,264,256]{2,1,0:T(8,128)(2,1)} %collective-permute-done.2.refs_2_), channel_id=1, source_target_pairs={{0,64},{16,80},{32,96},{48,112},{64,128},{80,144},{96,160},{112,17... | collective-permute-start | bytes 1622024 | tf_op jit(solution)/shard_map/ppermute | solution.py:198
  63.0 1.0 copy-start.2
  65.5 1.2 %copy-start.3 = (f32[8,256,128]{2,1,0:T(8,128)S(1)}, f32[8,256,128]{2,1,0:T(8,128)}, u32[]{:S(2)}) copy-start(f32[8,256,128]{2,1,0:T(8,128)} %copy-done.2) | copy-start | bytes 3145732
